TPU v7x, 32 devices: a whole 2x2x4 slice. The times are simulated.
32 devices in a mesh: corpus: 4 (over y, x), fsdp: 8 (over z, core).
Axes of the slice: x: 2, y: 2, z: 4, core: 2. Of those that a mesh axis runs over, the one named last changes fastest.
Arguments:
- inputs: bfloat16 [2048, 4096], P('fsdp', 'corpus'), may hold values from -128 to 128
- norm_gain: float32 [4096], replicated, may hold values from 0.1 to 1.9
- w_query: bfloat16 [4096, 8192], P('fsdp', 'corpus'), may hold values from -0.09375 to 0.09375
- w_key: bfloat16 [4096, 1024], P('fsdp', 'corpus'), may hold values from -0.09375 to 0.09375
- w_value: bfloat16 [4096, 1024], P('fsdp', 'corpus'), may hold values from -0.375 to 0.375
- query_bias: float32 [8192], P('corpus'), may hold values from -16 to 16
- key_bias: float32 [1024], P('corpus'), may hold values from -16 to 16
- value_bias: float32 [1024], P('corpus'), may hold values from -4 to 4
- key_cache: bfloat16 [8, 2048, 1024], P('fsdp', None, 'corpus'), may hold values from -16 to 16
- value_cache: bfloat16 [8, 2048, 1024], P('fsdp', None, 'corpus'), may hold values from -16 to 16
- source_doc: int32 [32], P('fsdp'), may hold values from 0 to 7, as said below
- prefix_len: int32 [32], P('fsdp'), may hold values from 1 to 2048
Outputs:
- attention: bfloat16 [2048, 8192], P('fsdp', 'corpus')
Inputs may be any that keep to these rules, and one draw needn't show every extreme that they name: `source_doc`: within the suffixes of one index of fsdp (aligned blocks of 4) no document appears more than 2 times, and one document, drawn from the seed, appears exactly 2 times in every such block.
All inputs are finite; a program needn't handle non-finite values.
Results may differ from a plain program's by a relative error of at most 0.0075.
The roundings to bfloat16 on the way count: a program that leaves them out, or rounds other values in their place, can miss the bound.
Values may be sent and summed in bfloat16 or wider, within the bound.
A program may use at most 128 MiB of HBM per device.

v0:
```python
import jax
import jax.numpy as jnp
from jax import lax
from jax.sharding import PartitionSpec as P

HD = 128
SL = 64
CAP = 2
EPS = 1e-06
THETA = 1000000.0
MASKED = -1e30


def rope_tables(position, width):
    half = width // 2
    freq = THETA ** (-(jnp.arange(half, dtype=jnp.float32) * 2.0 / width))
    angle = position.astype(jnp.float32)[..., None] * freq
    angle = jnp.concatenate([angle, angle], axis=-1)
    return (jnp.cos(angle), jnp.sin(angle))


def rotate(vector, cosine, sine):
    half = vector.shape[-1] // 2
    turned = jnp.concatenate([-vector[..., half:], vector[..., :half]], axis=-1)
    return vector * cosine + turned * sine


def normalize(rows, norm_gain):
    wide = rows.astype(jnp.float32)
    spread = jnp.mean(wide * wide, axis=-1, keepdims=True)
    return (wide * lax.rsqrt(spread + EPS) * norm_gain).astype(jnp.bfloat16)


def partial_attend(query, keys, values, live):
    count = query.shape[0]
    width = query.shape[2]
    length = keys.shape[0]
    kv_heads = keys.shape[1] // width
    group = query.shape[1] // kv_heads
    grouped = query.reshape(count, kv_heads, group, width)
    key_rows = keys.reshape(length, kv_heads, width)
    scores = jnp.einsum(
        "tkgd,lkd->tkgl", grouped, key_rows, preferred_element_type=jnp.float32
    ) * width ** (-0.5)
    scores = jnp.where(live[:, None, None, :], scores, MASKED)
    peak = jnp.max(scores, axis=-1)
    weights = jnp.exp(scores - peak[..., None])
    total = jnp.sum(weights, axis=-1)
    rounded = weights.astype(jnp.bfloat16)
    value_rows = values.reshape(length, kv_heads, width)
    weighted = jnp.einsum("tkgl,lkd->tkgd", rounded, value_rows, preferred_element_type=jnp.float32)
    return (
        weighted.reshape(count, kv_heads * group * width),
        peak.reshape(count, kv_heads * group),
        total.reshape(count, kv_heads * group),
    )


def settle(part):
    weighted, peak, total = part
    shape = peak.shape + (-1,)
    normed = (
        (weighted.reshape(shape) / total[..., None]).reshape(weighted.shape).astype(jnp.bfloat16)
    )
    return (normed, peak + jnp.log(total))


def combine(prefix_normed, prefix_lse, own):
    own_out, own_peak, own_total = own
    top = jnp.maximum(prefix_lse, own_peak)
    scale_first = jnp.exp(prefix_lse - top)
    scale_second = jnp.exp(own_peak - top)
    divisor = scale_first + own_total * scale_second
    shape = own_peak.shape + (-1,)
    mixed = (
        prefix_normed.astype(jnp.float32).reshape(shape) * scale_first[..., None]
        + own_out.reshape(shape) * scale_second[..., None]
    )
    mixed = mixed / divisor[..., None]
    return mixed.reshape(own_peak.shape[:-1] + (-1,)).astype(jnp.bfloat16)


def shards(
    inputs,
    norm_gain,
    w_query,
    w_key,
    w_value,
    query_bias,
    key_bias,
    value_bias,
    key_cache,
    value_cache,
    source_doc,
    prefix_len,
):
    full_rows = lax.all_gather(inputs, "corpus", axis=1, tiled=True)
    normed = normalize(full_rows, norm_gain)
    query_lin = jnp.dot(
        normed,
        lax.all_gather(w_query, "fsdp", axis=0, tiled=True),
        preferred_element_type=jnp.float32,
    )
    key_lin = jnp.dot(
        normed,
        lax.all_gather(w_key, "fsdp", axis=0, tiled=True),
        preferred_element_type=jnp.float32,
    )
    value_lin = jnp.dot(
        normed,
        lax.all_gather(w_value, "fsdp", axis=0, tiled=True),
        preferred_element_type=jnp.float32,
    )
    suffixes = source_doc.shape[0]
    width = HD
    q_heads = w_query.shape[1] // width
    kv_heads = w_key.shape[1] // width
    position = prefix_len[:, None] + jnp.arange(SL, dtype=jnp.int32)[None, :]
    cosine, sine = rope_tables(position, width)
    cosine = cosine[:, :, None, :]
    sine = sine[:, :, None, :]
    queries = rotate(
        (query_lin + query_bias).reshape(suffixes, SL, q_heads, width), cosine, sine
    ).astype(jnp.bfloat16)
    own_keys = rotate(
        (key_lin + key_bias).reshape(suffixes, SL, kv_heads, width), cosine, sine
    ).astype(jnp.bfloat16)
    own_keys = own_keys.reshape(suffixes, SL, kv_heads * width)
    own_values = (
        (value_lin + value_bias).astype(jnp.bfloat16).reshape(suffixes, SL, kv_heads * width)
    )
    causal = jnp.arange(SL, dtype=jnp.int32)[None, :] <= jnp.arange(SL, dtype=jnp.int32)[:, None]
    own_part = jax.vmap(partial_attend, in_axes=(0, 0, 0, None))(
        queries, own_keys, own_values, causal
    )
    documents = lax.axis_size("fsdp")
    slots = documents * CAP
    doc_length = key_cache.shape[1]
    order = jnp.arange(suffixes, dtype=jnp.int32)
    earlier = (source_doc[None, :] == source_doc[:, None]) & (order[None, :] < order[:, None])
    ranking = jnp.sum(earlier.astype(jnp.int32), axis=1)
    slot_of = source_doc * CAP + ranking
    matches = slot_of[None, :] == jnp.arange(slots, dtype=jnp.int32)[:, None]
    holder = jnp.sum(jnp.where(matches, order[None, :], 0), axis=1)
    occupied = jnp.any(matches, axis=1)
    slot_length = jnp.where(occupied, jnp.take(prefix_len, holder, axis=0), 0)
    slot_mask = (jnp.arange(doc_length, dtype=jnp.int32)[None, :] < slot_length[:, None]).astype(
        jnp.bfloat16
    )
    slot_queries = jnp.take(queries, holder, axis=0)
    initial = (
        jnp.zeros((suffixes, SL, q_heads * width), jnp.float32),
        jnp.zeros((suffixes, SL, q_heads), jnp.float32),
        jnp.zeros((suffixes, SL, q_heads), jnp.float32),
    )
    key_piece = lax.all_gather(key_cache, "fsdp", axis=0, tiled=True)
    value_piece = lax.all_gather(value_cache, "fsdp", axis=0, tiled=True)
    count = key_piece.shape[0]

    def one_document(item):
        doc_queries, doc_masks, doc_keys, doc_values = item
        live = jnp.broadcast_to(doc_masks[:, None, :] > 0, (CAP, SL, doc_masks.shape[-1]))
        return jax.vmap(partial_attend, in_axes=(0, None, None, 0))(
            doc_queries, doc_keys, doc_values, live
        )

    results = lax.map(
        one_document,
        (
            slot_queries.reshape((count, CAP) + slot_queries.shape[1:]),
            slot_mask.reshape(count, CAP, doc_length),
            key_piece,
            value_piece,
        ),
    )
    results = tuple((part.reshape((count * CAP,) + part.shape[2:]) for part in results))
    inside = (slot_of >= 0) & (slot_of < count * CAP)
    chosen = jnp.clip(slot_of, 0, count * CAP - 1)
    gathered_part = tuple(
        (
            jnp.where(inside[:, None, None], jnp.take(fresh, chosen, axis=0), older)
            for older, fresh in zip(initial, results)
        )
    )
    prefix_normed, prefix_lse = settle(gathered_part)
    attention = combine(prefix_normed, prefix_lse, own_part)
    return attention.reshape(suffixes * SL, q_heads * width)


def solution(mesh):
    in_specs = (
        P("fsdp", "corpus"),
        P(),
        P("fsdp", "corpus"),
        P("fsdp", "corpus"),
        P("fsdp", "corpus"),
        P("corpus"),
        P("corpus"),
        P("corpus"),
        P("fsdp", None, "corpus"),
        P("fsdp", None, "corpus"),
        P("fsdp"),
        P("fsdp"),
    )
    out_specs = P("fsdp", "corpus")
    return jax.shard_map(shards, mesh=mesh, in_specs=in_specs, out_specs=out_specs, check_vma=False)
```

profile of v0, /device:TPU:0, one launch (start us, length us, event | category | flops | bytes accessed | tf_op | source)
XLA Modules:
  0.0 685.7 jit_solution(6007420988527938023)
XLA Ops:
  15.4 31.9 %all-gather.11.cloned.1.call-done = bf16[256,4096]{1,0:T(8,128)(2,1)} async-done(((bf16[256,1024]{1,0:T(8,128)(2,1)}), bf16[256,4096]{1,0:T(8,128)(2,1)}) %all-gather.11.cloned.1.call-update) | async-done | bytes 2097168 | tf_op jit(solution)/shard_map/all_gather | solution.py:97
  47.3 2.2 fusion.13
  49.5 28.5 %all-gather.15.cloned.1.call-done = bf16[4096,256]{1,0:T(8,128)(2,1)} async-done(((bf16[512,256]{1,0:T(8,128)(2,1)}), bf16[4096,256]{1,0:T(8,128)(2,1)}) %all-gather.15.cloned.1.call-update) | async-done | bytes 2097168 | tf_op jit(solution)/shard_map/all_gather | solution.py:106
  78.0 2.4 convolution_add_fusion.2
  80.5 27.7 %all-gather.17.cloned.1.call-done = bf16[4096,256]{1,0:T(8,128)(2,1)} async-done(((bf16[512,256]{1,0:T(8,128)(2,1)}), bf16[4096,256]{1,0:T(8,128)(2,1)}) %all-gather.17.cloned.1.call-update) | async-done | bytes 2097168 | tf_op jit(solution)/shard_map/all_gather | solution.py:111
  108.2 2.4 fusion.27
  110.8 149.5 %all-gather.13.cloned.1.call-done = bf16[4096,2048]{1,0:T(8,128)(2,1)} async-done(((bf16[512,2048]{1,0:T(8,128)(2,1)}), bf16[4096,2048]{1,0:T(8,128)(2,1)}) %all-gather.13.cloned.1.call-update) | async-done | bytes 16777232 | tf_op jit(solution)/shard_map/all_gather | solution.py:101
  260.3 8.2 %fusion.26 = f32[32,8,16,128]{3,1,2,0:T(8,128)S(1)} fusion(bf16[4096,2048]{1,0:T(8,128)(2,1)} %all-gather.13.cloned.1.call-done, f32[2048]{0:T(1024)S(1)} %copy-done.18, bf16[256,4096]{1,0:T(8,128)(2,1)S(1)} %copy-done.7, f32[4096]{0:T(1024)S(1)} %copy-done.17, f32[256]{0:T(256)S(1)} %add_rsqrt_fusion), kind=kOutput, calls=%fused_computation.52 | convolution fusion | flops 4299685888 | bytes 20997120 | tf_op jit(solution)/shard_map/dot_general | solution.py:99
  272.3 1.6 fusion.56
  275.3 2.5 copy.105
  277.8 2.7 reshape.216
  280.5 3.0 fusion.20
  283.5 3.0 gather_fusion.1
  287.0 4.6 broadcast_select_fusion
  291.7 50.4 %all-gather.9.cloned.1.call-done = bf16[8,2048,256]{2,1,0:T(8,128)(2,1)} async-done(((bf16[1,2048,256]{2,1,0:T(8,128)(2,1)}), bf16[8,2048,256]{2,1,0:T(8,128)(2,1)}) %all-gather.9.cloned.1.call-update) | async-done | bytes 8388624 | tf_op jit(solution)/shard_map/all_gather | solution.py:156
  342.1 82.1 %all-gather.7.cloned.1.call-done = bf16[8,2048,256]{2,1,0:T(8,128)(2,1)} async-done(((bf16[1,2048,256]{2,1,0:T(8,128)(2,1)}), bf16[8,2048,256]{2,1,0:T(8,128)(2,1)}) %all-gather.7.cloned.1.call-update) | async-done | bytes 8388624 | tf_op jit(solution)/shard_map/all_gather | solution.py:157
  424.2 241.4 %while.14 = (s32[]{:T(128)}, f32[8,2,64,2048]{3,2,1,0:T(8,128)}, f32[8,2,64,16]{2,3,1,0:T(8,128)S(1)}, f32[8,2,64,16]{2,3,1,0:T(8,128)S(1)}, bf16[8,2048,256]{2,...) while((s32[]{:T(128)}, f32[8,2,64,2048]{3,2,1,0:T(8,128)}, ...), condition=%wide.region_7.8_spmd, body=%wide.region_4.0_spmd.sunk | while | flops 2193620992 | bytes 74047632 | solution.py:167
  428.5 1.4 copy.160
  429.9 7.1 %fusion.71 = (f32[2,64,2,8]{1,3,0,2:T(8,128)S(1)}, f32[2,2048,2,64,8]{1,3,4,2,0:T(8,128)}) fusion(pred[2,2048]{1,0:T(4,128)(4,1)S(1)} %compare_bitcast_fusion.2, bf16[2048,2,128,1,1]{0,2,4,3,1:T(8,128)(2,1)S(1)} %bitcast.138, bf16[2,64,2,8,128]{4,3,2,1,0:T(8,128)(2,1)S(1)} %dynamic-slice_bitcast_fusion.2), kind=kOutput, calls=%fused_computation.9.clone.1 | convolution fusion | flops 1086322688 | bytes 18362368 | tf_op jit(solution)/shard_map/while/body/eval_jaxpr/vmap(tkgd,lkd->tkgl)/dot_general | solution.py:42
  437.1 7.6 %fusion.72 = f32[2,64,2,8,128]{4,1,3,0,2:T(8,128)S(1)} fusion(bf16[2048,2,128,1,1]{0,2,4,3,1:T(8,128)(2,1)S(1)} %bitcast.142, f32[2,2048,2,64,8]{1,3,4,2,0:T(8,128)} %get-tuple-element.168, f32[2,64,2,8]{1,3,0,2:T(8,128)S(1)} %get-tuple-element.169, pred[2,2048]{1,0:T(4,128)(4,1)S(1)} %compare_bitcast_fusion.2), kind=kOutput, calls=%fused_computation.12.clone.1 | convolution fusion | flops 1090519040 | bytes 18886656 | tf_op jit(solution)/shard_map/while/body/eval_jaxpr/vmap(tkgl,lkd->tkgd)/dot_general | solution.py:51
  444.6 7.8 %fusion.73 = f32[2,64,2,8]{1,3,0,2:T(8,128)S(1)} fusion(f32[2,2048,2,64,8]{1,3,4,2,0:T(8,128)} %get-tuple-element.168, f32[2,64,2,8]{1,3,0,2:T(8,128)S(1)} %get-tuple-element.169, pred[2,2048]{1,0:T(4,128)(4,1)S(1)} %compare_bitcast_fusion.2), kind=kLoop, calls=%fused_computation.7.clone.1 | loop fusion | flops 16775168 | bytes 16797696 | tf_op jit(solution)/shard_map/while/body/eval_jaxpr/vmap()/reduce_sum | solution.py:48
  460.1 7.1 %fusion.71 = (f32[2,64,2,8]{1,3,0,2:T(8,128)S(1)}, f32[2,2048,2,64,8]{1,3,4,2,0:T(8,128)}) fusion(pred[2,2048]{1,0:T(4,128)(4,1)S(1)} %compare_bitcast_fusion.2, bf16[2048,2,128,1,1]{0,2,4,3,1:T(8,128)(2,1)S(1)} %bitcast.138, bf16[2,64,2,8,128]{4,3,2,1,0:T(8,128)(2,1)S(1)} %dynamic-slice_bitcast_fusion.2), kind=kOutput, calls=%fused_computation.9.clone.1 | convolution fusion | flops 1086322688 | bytes 18362368 | tf_op jit(solution)/shard_map/while/body/eval_jaxpr/vmap(tkgd,lkd->tkgl)/dot_general | solution.py:42
  467.2 7.6 %fusion.72 = f32[2,64,2,8,128]{4,1,3,0,2:T(8,128)S(1)} fusion(bf16[2048,2,128,1,1]{0,2,4,3,1:T(8,128)(2,1)S(1)} %bitcast.142, f32[2,2048,2,64,8]{1,3,4,2,0:T(8,128)} %get-tuple-element.168, f32[2,64,2,8]{1,3,0,2:T(8,128)S(1)} %get-tuple-element.169, pred[2,2048]{1,0:T(4,128)(4,1)S(1)} %compare_bitcast_fusion.2), kind=kOutput, calls=%fused_computation.12.clone.1 | convolution fusion | flops 1090519040 | bytes 18886656 | tf_op jit(solution)/shard_map/while/body/eval_jaxpr/vmap(tkgl,lkd->tkgd)/dot_general | solution.py:51
  474.8 7.8 %fusion.73 = f32[2,64,2,8]{1,3,0,2:T(8,128)S(1)} fusion(f32[2,2048,2,64,8]{1,3,4,2,0:T(8,128)} %get-tuple-element.168, f32[2,64,2,8]{1,3,0,2:T(8,128)S(1)} %get-tuple-element.169, pred[2,2048]{1,0:T(4,128)(4,1)S(1)} %compare_bitcast_fusion.2), kind=kLoop, calls=%fused_computation.7.clone.1 | loop fusion | flops 16775168 | bytes 16797696 | tf_op jit(solution)/shard_map/while/body/eval_jaxpr/vmap()/reduce_sum | solution.py:48
  488.8 1.4 copy.160
  490.3 7.1 %fusion.71 = (f32[2,64,2,8]{1,3,0,2:T(8,128)S(1)}, f32[2,2048,2,64,8]{1,3,4,2,0:T(8,128)}) fusion(pred[2,2048]{1,0:T(4,128)(4,1)S(1)} %compare_bitcast_fusion.2, bf16[2048,2,128,1,1]{0,2,4,3,1:T(8,128)(2,1)S(1)} %bitcast.138, bf16[2,64,2,8,128]{4,3,2,1,0:T(8,128)(2,1)S(1)} %dynamic-slice_bitcast_fusion.2), kind=kOutput, calls=%fused_computation.9.clone.1 | convolution fusion | flops 1086322688 | bytes 18362368 | tf_op jit(solution)/shard_map/while/body/eval_jaxpr/vmap(tkgd,lkd->tkgl)/dot_general | solution.py:42
  497.4 7.6 %fusion.72 = f32[2,64,2,8,128]{4,1,3,0,2:T(8,128)S(1)} fusion(bf16[2048,2,128,1,1]{0,2,4,3,1:T(8,128)(2,1)S(1)} %bitcast.142, f32[2,2048,2,64,8]{1,3,4,2,0:T(8,128)} %get-tuple-element.168, f32[2,64,2,8]{1,3,0,2:T(8,128)S(1)} %get-tuple-element.169, pred[2,2048]{1,0:T(4,128)(4,1)S(1)} %compare_bitcast_fusion.2), kind=kOutput, calls=%fused_computation.12.clone.1 | convolution fusion | flops 1090519040 | bytes 18886656 | tf_op jit(solution)/shard_map/while/body/eval_jaxpr/vmap(tkgl,lkd->tkgd)/dot_general | solution.py:51
  505.0 7.8 %fusion.73 = f32[2,64,2,8]{1,3,0,2:T(8,128)S(1)} fusion(f32[2,2048,2,64,8]{1,3,4,2,0:T(8,128)} %get-tuple-element.168, f32[2,64,2,8]{1,3,0,2:T(8,128)S(1)} %get-tuple-element.169, pred[2,2048]{1,0:T(4,128)(4,1)S(1)} %compare_bitcast_fusion.2), kind=kLoop, calls=%fused_computation.7.clone.1 | loop fusion | flops 16775168 | bytes 16797696 | tf_op jit(solution)/shard_map/while/body/eval_jaxpr/vmap()/reduce_sum | solution.py:48
  519.0 1.4 copy.160
  520.4 7.1 %fusion.71 = (f32[2,64,2,8]{1,3,0,2:T(8,128)S(1)}, f32[2,2048,2,64,8]{1,3,4,2,0:T(8,128)}) fusion(pred[2,2048]{1,0:T(4,128)(4,1)S(1)} %compare_bitcast_fusion.2, bf16[2048,2,128,1,1]{0,2,4,3,1:T(8,128)(2,1)S(1)} %bitcast.138, bf16[2,64,2,8,128]{4,3,2,1,0:T(8,128)(2,1)S(1)} %dynamic-slice_bitcast_fusion.2), kind=kOutput, calls=%fused_computation.9.clone.1 | convolution fusion | flops 1086322688 | bytes 18362368 | tf_op jit(solution)/shard_map/while/body/eval_jaxpr/vmap(tkgd,lkd->tkgl)/dot_general | solution.py:42
  527.6 7.6 %fusion.72 = f32[2,64,2,8,128]{4,1,3,0,2:T(8,128)S(1)} fusion(bf16[2048,2,128,1,1]{0,2,4,3,1:T(8,128)(2,1)S(1)} %bitcast.142, f32[2,2048,2,64,8]{1,3,4,2,0:T(8,128)} %get-tuple-element.168, f32[2,64,2,8]{1,3,0,2:T(8,128)S(1)} %get-tuple-element.169, pred[2,2048]{1,0:T(4,128)(4,1)S(1)} %compare_bitcast_fusion.2), kind=kOutput, calls=%fused_computation.12.clone.1 | convolution fusion | flops 1090519040 | bytes 18886656 | tf_op jit(solution)/shard_map/while/body/eval_jaxpr/vmap(tkgl,lkd->tkgd)/dot_general | solution.py:51
  535.1 7.8 %fusion.73 = f32[2,64,2,8]{1,3,0,2:T(8,128)S(1)} fusion(f32[2,2048,2,64,8]{1,3,4,2,0:T(8,128)} %get-tuple-element.168, f32[2,64,2,8]{1,3,0,2:T(8,128)S(1)} %get-tuple-element.169, pred[2,2048]{1,0:T(4,128)(4,1)S(1)} %compare_bitcast_fusion.2), kind=kLoop, calls=%fused_computation.7.clone.1 | loop fusion | flops 16775168 | bytes 16797696 | tf_op jit(solution)/shard_map/while/body/eval_jaxpr/vmap()/reduce_sum | solution.py:48
  550.6 7.1 %fusion.71 = (f32[2,64,2,8]{1,3,0,2:T(8,128)S(1)}, f32[2,2048,2,64,8]{1,3,4,2,0:T(8,128)}) fusion(pred[2,2048]{1,0:T(4,128)(4,1)S(1)} %compare_bitcast_fusion.2, bf16[2048,2,128,1,1]{0,2,4,3,1:T(8,128)(2,1)S(1)} %bitcast.138, bf16[2,64,2,8,128]{4,3,2,1,0:T(8,128)(2,1)S(1)} %dynamic-slice_bitcast_fusion.2), kind=kOutput, calls=%fused_computation.9.clone.1 | convolution fusion | flops 1086322688 | bytes 18362368 | tf_op jit(solution)/shard_map/while/body/eval_jaxpr/vmap(tkgd,lkd->tkgl)/dot_general | solution.py:42
  557.7 7.6 %fusion.72 = f32[2,64,2,8,128]{4,1,3,0,2:T(8,128)S(1)} fusion(bf16[2048,2,128,1,1]{0,2,4,3,1:T(8,128)(2,1)S(1)} %bitcast.142, f32[2,2048,2,64,8]{1,3,4,2,0:T(8,128)} %get-tuple-element.168, f32[2,64,2,8]{1,3,0,2:T(8,128)S(1)} %get-tuple-element.169, pred[2,2048]{1,0:T(4,128)(4,1)S(1)} %compare_bitcast_fusion.2), kind=kOutput, calls=%fused_computation.12.clone.1 | convolution fusion | flops 1090519040 | bytes 18886656 | tf_op jit(solution)/shard_map/while/body/eval_jaxpr/vmap(tkgl,lkd->tkgd)/dot_general | solution.py:51
  565.3 7.8 %fusion.73 = f32[2,64,2,8]{1,3,0,2:T(8,128)S(1)} fusion(f32[2,2048,2,64,8]{1,3,4,2,0:T(8,128)} %get-tuple-element.168, f32[2,64,2,8]{1,3,0,2:T(8,128)S(1)} %get-tuple-element.169, pred[2,2048]{1,0:T(4,128)(4,1)S(1)} %compare_bitcast_fusion.2), kind=kLoop, calls=%fused_computation.7.clone.1 | loop fusion | flops 16775168 | bytes 16797696 | tf_op jit(solution)/shard_map/while/body/eval_jaxpr/vmap()/reduce_sum | solution.py:48
  579.4 1.4 copy.160
  580.8 7.1 %fusion.71 = (f32[2,64,2,8]{1,3,0,2:T(8,128)S(1)}, f32[2,2048,2,64,8]{1,3,4,2,0:T(8,128)}) fusion(pred[2,2048]{1,0:T(4,128)(4,1)S(1)} %compare_bitcast_fusion.2, bf16[2048,2,128,1,1]{0,2,4,3,1:T(8,128)(2,1)S(1)} %bitcast.138, bf16[2,64,2,8,128]{4,3,2,1,0:T(8,128)(2,1)S(1)} %dynamic-slice_bitcast_fusion.2), kind=kOutput, calls=%fused_computation.9.clone.1 | convolution fusion | flops 1086322688 | bytes 18362368 | tf_op jit(solution)/shard_map/while/body/eval_jaxpr/vmap(tkgd,lkd->tkgl)/dot_general | solution.py:42
  587.9 7.6 %fusion.72 = f32[2,64,2,8,128]{4,1,3,0,2:T(8,128)S(1)} fusion(bf16[2048,2,128,1,1]{0,2,4,3,1:T(8,128)(2,1)S(1)} %bitcast.142, f32[2,2048,2,64,8]{1,3,4,2,0:T(8,128)} %get-tuple-element.168, f32[2,64,2,8]{1,3,0,2:T(8,128)S(1)} %get-tuple-element.169, pred[2,2048]{1,0:T(4,128)(4,1)S(1)} %compare_bitcast_fusion.2), kind=kOutput, calls=%fused_computation.12.clone.1 | convolution fusion | flops 1090519040 | bytes 18886656 | tf_op jit(solution)/shard_map/while/body/eval_jaxpr/vmap(tkgl,lkd->tkgd)/dot_general | solution.py:51
  595.5 7.8 %fusion.73 = f32[2,64,2,8]{1,3,0,2:T(8,128)S(1)} fusion(f32[2,2048,2,64,8]{1,3,4,2,0:T(8,128)} %get-tuple-element.168, f32[2,64,2,8]{1,3,0,2:T(8,128)S(1)} %get-tuple-element.169, pred[2,2048]{1,0:T(4,128)(4,1)S(1)} %compare_bitcast_fusion.2), kind=kLoop, calls=%fused_computation.7.clone.1 | loop fusion | flops 16775168 | bytes 16797696 | tf_op jit(solution)/shard_map/while/body/eval_jaxpr/vmap()/reduce_sum | solution.py:48
  611.0 7.1 %fusion.71 = (f32[2,64,2,8]{1,3,0,2:T(8,128)S(1)}, f32[2,2048,2,64,8]{1,3,4,2,0:T(8,128)}) fusion(pred[2,2048]{1,0:T(4,128)(4,1)S(1)} %compare_bitcast_fusion.2, bf16[2048,2,128,1,1]{0,2,4,3,1:T(8,128)(2,1)S(1)} %bitcast.138, bf16[2,64,2,8,128]{4,3,2,1,0:T(8,128)(2,1)S(1)} %dynamic-slice_bitcast_fusion.2), kind=kOutput, calls=%fused_computation.9.clone.1 | convolution fusion | flops 1086322688 | bytes 18362368 | tf_op jit(solution)/shard_map/while/body/eval_jaxpr/vmap(tkgd,lkd->tkgl)/dot_general | solution.py:42
  618.1 7.6 %fusion.72 = f32[2,64,2,8,128]{4,1,3,0,2:T(8,128)S(1)} fusion(bf16[2048,2,128,1,1]{0,2,4,3,1:T(8,128)(2,1)S(1)} %bitcast.142, f32[2,2048,2,64,8]{1,3,4,2,0:T(8,128)} %get-tuple-element.168, f32[2,64,2,8]{1,3,0,2:T(8,128)S(1)} %get-tuple-element.169, pred[2,2048]{1,0:T(4,128)(4,1)S(1)} %compare_bitcast_fusion.2), kind=kOutput, calls=%fused_computation.12.clone.1 | convolution fusion | flops 1090519040 | bytes 18886656 | tf_op jit(solution)/shard_map/while/body/eval_jaxpr/vmap(tkgl,lkd->tkgd)/dot_general | solution.py:51
  625.7 7.8 %fusion.73 = f32[2,64,2,8]{1,3,0,2:T(8,128)S(1)} fusion(f32[2,2048,2,64,8]{1,3,4,2,0:T(8,128)} %get-tuple-element.168, f32[2,64,2,8]{1,3,0,2:T(8,128)S(1)} %get-tuple-element.169, pred[2,2048]{1,0:T(4,128)(4,1)S(1)} %compare_bitcast_fusion.2), kind=kLoop, calls=%fused_computation.7.clone.1 | loop fusion | flops 16775168 | bytes 16797696 | tf_op jit(solution)/shard_map/while/body/eval_jaxpr/vmap()/reduce_sum | solution.py:48
  639.7 1.4 copy.160
  641.1 7.1 %fusion.71 = (f32[2,64,2,8]{1,3,0,2:T(8,128)S(1)}, f32[2,2048,2,64,8]{1,3,4,2,0:T(8,128)}) fusion(pred[2,2048]{1,0:T(4,128)(4,1)S(1)} %compare_bitcast_fusion.2, bf16[2048,2,128,1,1]{0,2,4,3,1:T(8,128)(2,1)S(1)} %bitcast.138, bf16[2,64,2,8,128]{4,3,2,1,0:T(8,128)(2,1)S(1)} %dynamic-slice_bitcast_fusion.2), kind=kOutput, calls=%fused_computation.9.clone.1 | convolution fusion | flops 1086322688 | bytes 18362368 | tf_op jit(solution)/shard_map/while/body/eval_jaxpr/vmap(tkgd,lkd->tkgl)/dot_general | solution.py:42
  648.2 7.6 %fusion.72 = f32[2,64,2,8,128]{4,1,3,0,2:T(8,128)S(1)} fusion(bf16[2048,2,128,1,1]{0,2,4,3,1:T(8,128)(2,1)S(1)} %bitcast.142, f32[2,2048,2,64,8]{1,3,4,2,0:T(8,128)} %get-tuple-element.168, f32[2,64,2,8]{1,3,0,2:T(8,128)S(1)} %get-tuple-element.169, pred[2,2048]{1,0:T(4,128)(4,1)S(1)} %compare_bitcast_fusion.2), kind=kOutput, calls=%fused_computation.12.clone.1 | convolution fusion | flops 1090519040 | bytes 18886656 | tf_op jit(solution)/shard_map/while/body/eval_jaxpr/vmap(tkgl,lkd->tkgd)/dot_general | solution.py:51
  655.8 7.8 %fusion.73 = f32[2,64,2,8]{1,3,0,2:T(8,128)S(1)} fusion(f32[2,2048,2,64,8]{1,3,4,2,0:T(8,128)} %get-tuple-element.168, f32[2,64,2,8]{1,3,0,2:T(8,128)S(1)} %get-tuple-element.169, pred[2,2048]{1,0:T(4,128)(4,1)S(1)} %compare_bitcast_fusion.2), kind=kLoop, calls=%fused_computation.7.clone.1 | loop fusion | flops 16775168 | bytes 16797696 | tf_op jit(solution)/shard_map/while/body/eval_jaxpr/vmap()/reduce_sum | solution.py:48
  666.2 4.2 gather_fusion.2
  674.5 4.4 fusion.16
  (191 shorter events, 73.0 us)
Async XLA Ops:
  6.5 40.7 %all-gather.11.cloned.1.call-start = ((), (), s32[]{:S(2)}) async-start(), calls=%async_computation.2 | async-start | bytes 2621440 | tf_op jit(solution)/shard_map/all_gather | solution.py:97
  7.3 70.7 %all-gather.15.cloned.1.call-start = ((), (), s32[]{:S(2)}) async-start(), calls=%async_computation.4 | async-start | bytes 2359296 | tf_op jit(solution)/shard_map/all_gather | solution.py:106
  8.0 100.2 %all-gather.17.cloned.1.call-start = ((), (), s32[]{:S(2)}) async-start(), calls=%async_computation.5 | async-start | bytes 2359296 | tf_op jit(solution)/shard_map/all_gather | solution.py:111
  8.7 1.8 copy-start.16
  8.8 4.3 copy-start
  8.8 251.5 %all-gather.13.cloned.1.call-start = ((), (), s32[]{:S(2)}) async-start(), calls=%async_computation.3 | async-start | bytes 18874368 | tf_op jit(solution)/shard_map/all_gather | solution.py:101
  9.3 332.7 %all-gather.9.cloned.1.call-start = ((), (), s32[]{:S(2)}) async-start(), calls=%async_computation.1 | async-start | bytes 9437184 | tf_op jit(solution)/shard_map/all_gather | solution.py:156
  9.9 68.1 %copy-start.17 = (f32[4096]{0:T(1024)S(1)}, f32[4096]{0:T(1024)}, u32[]{:S(2)}) copy-start(f32[4096]{0:T(1024)} %param.17) | copy-start | bytes 49156
  9.9 68.1 %copy-start.19 = (f32[256]{0:T(256)S(1)}, f32[256]{0:T(256)}, u32[]{:S(2)}) copy-start(f32[256]{0:T(256)} %param.22) | copy-start | bytes 3076
  9.9 414.2 %all-gather.7.cloned.1.call-start = ((), (), s32[]{:S(2)}) async-start(), calls=%async_computation | async-start | bytes 9437184 | tf_op jit(solution)/shard_map/all_gather | solution.py:157
  10.8 0.5 copy-start.10
  12.2 3.2 copy-start.14
  47.3 30.7 %copy-start.7 = (bf16[256,4096]{1,0:T(8,128)(2,1)S(1)}, bf16[256,4096]{1,0:T(8,128)(2,1)}, u32[]{:S(2)}) copy-start(bf16[256,4096]{1,0:T(8,128)(2,1)} %all-gather.11.cloned.1.call-done) | copy-start | bytes 6291460
  49.5 58.7 %copy-start.20 = (f32[256]{0:T(256)S(1)}, f32[256]{0:T(256)}, u32[]{:S(2)}) copy-start(f32[256]{0:T(256)} %param.23) | copy-start | bytes 3076
  80.5 179.8 %copy-start.18 = (f32[2048]{0:T(1024)S(1)}, f32[2048]{0:T(1024)}, u32[]{:S(2)}) copy-start(f32[2048]{0:T(1024)} %param.21) | copy-start | bytes 24580
  269.6 1.3 copy-start.4
  269.6 2.0 copy-start.5
  273.9 1.4 copy-start.2
  283.5 3.0 copy-start.3
  287.0 137.1 %copy-start.8 = (f32[8,2,64,16]{2,3,1,0:T(8,128)S(1)}, f32[8,2,64,16]{2,3,1,0:T(8,128)}, u32[]{:S(2)}) copy-start(f32[8,2,64,16]{2,3,1,0:T(8,128)} %custom-call.12) | copy-start | bytes 196612
  287.0 137.1 %copy-start.9 = (f32[8,2,64,16]{2,3,1,0:T(8,128)S(1)}, f32[8,2,64,16]{2,3,1,0:T(8,128)}, u32[]{:S(2)}) copy-start(f32[8,2,64,16]{2,3,1,0:T(8,128)} %custom-call.11) | copy-start | bytes 196612
  429.9 7.1 %copy-start.1 = (bf16[1,2048,256]{1,2,0:T(8,128)(2,1)S(1)}, bf16[1,2048,256]{1,2,0:T(8,128)(2,1)}, u32[]{:S(2)}) copy-start(bf16[1,2048,256]{1,2,0:T(8,128)(2,1)} %copy.160) | copy-start | bytes 3145732 | tf_op jit(solution)/shard_map/while
  460.1 7.1 %copy-start.1 = (bf16[1,2048,256]{1,2,0:T(8,128)(2,1)S(1)}, bf16[1,2048,256]{1,2,0:T(8,128)(2,1)}, u32[]{:S(2)}) copy-start(bf16[1,2048,256]{1,2,0:T(8,128)(2,1)} %copy.160) | copy-start | bytes 3145732 | tf_op jit(solution)/shard_map/while
  490.3 7.1 %copy-start.1 = (bf16[1,2048,256]{1,2,0:T(8,128)(2,1)S(1)}, bf16[1,2048,256]{1,2,0:T(8,128)(2,1)}, u32[]{:S(2)}) copy-start(bf16[1,2048,256]{1,2,0:T(8,128)(2,1)} %copy.160) | copy-start | bytes 3145732 | tf_op jit(solution)/shard_map/while
  520.4 7.1 %copy-start.1 = (bf16[1,2048,256]{1,2,0:T(8,128)(2,1)S(1)}, bf16[1,2048,256]{1,2,0:T(8,128)(2,1)}, u32[]{:S(2)}) copy-start(bf16[1,2048,256]{1,2,0:T(8,128)(2,1)} %copy.160) | copy-start | bytes 3145732 | tf_op jit(solution)/shard_map/while
  550.6 7.1 %copy-start.1 = (bf16[1,2048,256]{1,2,0:T(8,128)(2,1)S(1)}, bf16[1,2048,256]{1,2,0:T(8,128)(2,1)}, u32[]{:S(2)}) copy-start(bf16[1,2048,256]{1,2,0:T(8,128)(2,1)} %copy.160) | copy-start | bytes 3145732 | tf_op jit(solution)/shard_map/while
  580.8 7.1 %copy-start.1 = (bf16[1,2048,256]{1,2,0:T(8,128)(2,1)S(1)}, bf16[1,2048,256]{1,2,0:T(8,128)(2,1)}, u32[]{:S(2)}) copy-start(bf16[1,2048,256]{1,2,0:T(8,128)(2,1)} %copy.160) | copy-start | bytes 3145732 | tf_op jit(solution)/shard_map/while
  611.0 7.1 %copy-start.1 = (bf16[1,2048,256]{1,2,0:T(8,128)(2,1)S(1)}, bf16[1,2048,256]{1,2,0:T(8,128)(2,1)}, u32[]{:S(2)}) copy-start(bf16[1,2048,256]{1,2,0:T(8,128)(2,1)} %copy.160) | copy-start | bytes 3145732 | tf_op jit(solution)/shard_map/while
  641.1 7.1 %copy-start.1 = (bf16[1,2048,256]{1,2,0:T(8,128)(2,1)S(1)}, bf16[1,2048,256]{1,2,0:T(8,128)(2,1)}, u32[]{:S(2)}) copy-start(bf16[1,2048,256]{1,2,0:T(8,128)(2,1)} %copy.160) | copy-start | bytes 3145732 | tf_op jit(solution)/shard_map/while
  666.2 4.9 copy-start.11
  666.2 4.9 copy-start.15
  672.9 1.6 copy-start.6
  672.9 1.6 copy-start.12
  672.9 1.6 copy-start.13
Sparse Core Ops, SparseCore 0:
  9.2 38.0 all-gather.10
  48.8 29.0 all-gather.14
  79.6 28.5 all-gather.16
  109.7 150.5 all-gather.12
  261.7 80.2 all-gather.8
  343.5 80.5 all-gather.6
where the time goes:
time: 687 us; the launch traced here: 686 us
  waiting for transfers between devices  374 us (54%)
  matrix products  133 us (19%)
  local copies, waits for them, and re-layouts  84.7 us (12%)
  other arithmetic  80.2 us (12%)
  between operations  13.9 us (2%)
    all_gather x1, waiting for transfers between devices, shards(): lax.all_gather(w_query, 'fsdp', axis=0, tiled=True)  150 us
    all_gather x1, waiting for transfers between devices, shards(): value_piece = lax.all_gather(value_cache, 'fsdp', axis=0, tiled=True)  82.1 us
    reduce_sum x9, other arithmetic, partial_attend(): total = jnp.sum(weights, axis=-1)  63 us
    dot_general x9, matrix products, partial_attend(): jnp.einsum('tkgl,lkd->tkgd', rounded, value_rows, preferred_element_type=...  61.1 us
    dot_general x9, matrix products, partial_attend(): jnp.einsum('tkgd,lkd->tkgl', grouped, key_rows, preferred_element_type=jn...  58.6 us
    all_gather x1, waiting for transfers between devices, shards(): key_piece = lax.all_gather(key_cache, 'fsdp', axis=0, tiled=True)  50.4 us
    dynamic_slice x32, local copies, waits for them, and re-layouts, shards(): lax.map(one_document, (slot_queries.reshape((count, CAP) + slot_queries.s...  37.3 us
    all_gather x1, waiting for transfers between devices, shards(): full_rows = lax.all_gather(inputs, 'corpus', axis=1, tiled=True)  31.9 us
  transfers between devices with their start and end apart: 6, of which 6 were waited for; matrix products, arithmetic and copies ran while one was open for 6% of the time, Pallas kernels for 0%

commit v1 on v0

--- a/solution.py
+++ b/solution.py
@@ -2,6 +2,7 @@
 import jax.numpy as jnp
 from jax import lax
 from jax.sharding import PartitionSpec as P
+from jax.lax import axis_index, axis_size, ppermute
 
 HD = 128
 SL = 64
@@ -9,6 +10,32 @@
 EPS = 1e-06
 THETA = 1000000.0
 MASKED = -1e30
+
+
+def advance_sample(w_in, which_dim):
+    w_in = jnp.moveaxis(w_in, 0, which_dim)
+    aux = w_in.shape
+    return w_in.reshape(
+        *aux[:which_dim], aux[which_dim] * aux[which_dim + 1], *aux[which_dim + 2 :]
+    )
+
+
+def panels_push(page, axis_id, axis_no):
+    chips = axis_size(axis_id)
+    sides = list(map(lambda j0: (j0, (j0 + 1) % chips), range(chips)))
+    blocks_here = [(k0, b) for b, k0 in sides]
+    a_next, local_part = ([], [])
+    for u in tuple(range(chips - 1)):
+        if u % 2 == 0:
+            a_next.append(ppermute(a_next[-1] if a_next else page, axis_id, perm=sides))
+        else:
+            local_part.append(
+                ppermute(local_part[-1] if local_part else page, axis_id, blocks_here)
+            )
+    side_arr = jnp.stack([*a_next[::-1], page, *local_part], axis=0)
+    extra = axis_index(axis_id) - len(a_next)
+    side_arr = side_arr[(jnp.arange(chips) - extra) % chips]
+    return advance_sample(side_arr, axis_no)
 
 
 def rope_tables(position, width):
@@ -96,11 +123,7 @@
 ):
     full_rows = lax.all_gather(inputs, "corpus", axis=1, tiled=True)
     normed = normalize(full_rows, norm_gain)
-    query_lin = jnp.dot(
-        normed,
-        lax.all_gather(w_query, "fsdp", axis=0, tiled=True),
-        preferred_element_type=jnp.float32,
-    )
+    query_lin = jnp.dot(normed, panels_push(w_query, "fsdp", 0), preferred_element_type=jnp.float32)
     key_lin = jnp.dot(
         normed,
         lax.all_gather(w_key, "fsdp", axis=0, tiled=True),

time: 687 us -> 567 us (0.83)
  waiting for transfers between devices: 374 us -> 260 us
  local copies, waits for them, and re-layouts: 84.7 us -> 128 us
  matrix products: 133 us -> 95.2 us
  other arithmetic: 80.2 us -> 56.7 us
  starting transfers between devices: 0.19 us -> 11.3 us
    ppermute x0 -> x7, waiting for transfers between devices: none -> 238 us  [the longest x4 238 us: panels_push(): a_next.append(ppermute(a_next[-1] if a_next else page, axis_id, perm=sides))]
    all_gather x1 -> x0, waiting for transfers between devices: 150 us -> none  [shards(): lax.all_gather(w_query, 'fsdp', axis=0, tiled=True)]
    all_gather x1, waiting for transfers between devices: 82.1 us -> 0.01 us  [shards(): value_piece = lax.all_gather(value_cache, 'fsdp', axis=0, tiled=True)]
    dot_general x9, matrix products: 58.6 us -> 23.9 us  [partial_attend(): jnp.einsum('tkgd,lkd->tkgl', grouped, key_rows, preferred_element_type=jn...]
    all_gather x1, waiting for transfers between devices: 31.9 us -> 0.02 us  [shards(): full_rows = lax.all_gather(inputs, 'corpus', axis=1, tiled=True)]
    reduce_sum x9, other arithmetic: 63 us -> 31.2 us  [partial_attend(): total = jnp.sum(weights, axis=-1)]
    all_gather x1, waiting for transfers between devices: 50.4 us -> 18.7 us  [shards(): key_piece = lax.all_gather(key_cache, 'fsdp', axis=0, tiled=True)]
    all_gather x1, waiting for transfers between devices: 28.5 us -> 0.02 us  [shards(): lax.all_gather(w_key, 'fsdp', axis=0, tiled=True)]
  transfers between devices with their start and end apart: 6 -> 12, of which waited for: 6 -> 5; matrix products, arithmetic and copies ran while one was open for 6% -> 14% of each run, Pallas kernels for 0% -> 0%
where the time goes in v1:
time: 567 us; the launch traced here: 566 us
  waiting for transfers between devices  260 us (46%)
  local copies, waits for them, and re-layouts  128 us (23%)
  matrix products  95.2 us (17%)
  other arithmetic  56.7 us (10%)
  between operations  13.7 us (2%)
  starting transfers between devices  11.3 us (2%)
    ppermute x4, waiting for transfers between devices, panels_push(): a_next.append(ppermute(a_next[-1] if a_next else page, axis_id, perm=sides))  238 us
    dot_general x9, matrix products, partial_attend(): jnp.einsum('tkgl,lkd->tkgd', rounded, value_rows, preferred_element_type=...  61 us
    reduce_sum x9, other arithmetic, partial_attend(): total = jnp.sum(weights, axis=-1)  31.2 us
    dynamic_slice x32, local copies, waits for them, and re-layouts, shards(): lax.map(one_document, (slot_queries.reshape((count, CAP) + slot_queries.s...  31 us
    dot_general x9, matrix products, partial_attend(): jnp.einsum('tkgd,lkd->tkgl', grouped, key_rows, preferred_element_type=jn...  23.9 us
    gather x3, local copies, waits for them, and re-layouts, panels_push(): side_arr = side_arr[(jnp.arange(chips) - extra) % chips]  23.7 us
    all_gather x1, waiting for transfers between devices, shards(): key_piece = lax.all_gather(key_cache, 'fsdp', axis=0, tiled=True)  18.7 us
    while x16, local copies, waits for them, and re-layouts  15.3 us
  transfers between devices with their start and end apart: 12, of which 5 were waited for; matrix products, arithmetic and copies ran while one was open for 14% of the time, Pallas kernels for 0%

profile of v1, /device:TPU:0, one launch (start us, length us, event | category | flops | bytes accessed | tf_op | source)
XLA Modules:
  0.0 565.7 jit_solution(3845225101653030087)
XLA Ops:
  9.9 27.9 %collective-permute-done = bf16[512,2048]{1,0:T(8,128)(2,1)} collective-permute-done((bf16[512,2048]{1,0:T(8,128)(2,1)S(1)}, bf16[512,2048]{1,0:T(8,128)(2,1)}, u32[]{:S(2)}, u32[]{:S(2)}) %collective-permute-start) | collective-permute-done | bytes 2097184 | tf_op jit(solution)/shard_map/ppermute | solution.py:30
  37.8 3.6 collective-permute-start.4
  41.4 62.7 %collective-permute-done.1 = bf16[512,2048]{1,0:T(8,128)(2,1)} collective-permute-done((bf16[512,2048]{1,0:T(8,128)(2,1)}, bf16[512,2048]{1,0:T(8,128)(2,1)}, u32[]{:S(2)}, u32[]{:S(2)}) %collective-permute-start.1) | collective-permute-done | bytes 2097184 | tf_op jit(solution)/shard_map/ppermute | solution.py:30
  108.2 3.6 collective-permute-start.5
  111.8 72.0 %collective-permute-done.2 = bf16[512,2048]{1,0:T(8,128)(2,1)} collective-permute-done((bf16[512,2048]{1,0:T(8,128)(2,1)}, bf16[512,2048]{1,0:T(8,128)(2,1)}, u32[]{:S(2)}, u32[]{:S(2)}) %collective-permute-start.2) | collective-permute-done | bytes 2097184 | tf_op jit(solution)/shard_map/ppermute | solution.py:30
  183.9 2.2 fusion.13
  186.2 2.4 convolution_add_fusion.2
  188.8 3.1 fusion.27
  192.1 3.5 collective-permute-start.6
  195.6 76.0 %collective-permute-done.3 = bf16[512,2048]{1,0:T(8,128)(2,1)} collective-permute-done((bf16[512,2048]{1,0:T(8,128)(2,1)}, bf16[512,2048]{1,0:T(8,128)(2,1)}, u32[]{:S(2)}, u32[]{:S(2)}) %collective-permute-start.3) | collective-permute-done | bytes 2097184 | tf_op jit(solution)/shard_map/ppermute | solution.py:30
  283.3 7.3 %fusion.58 = (bf16[8,512,1024]{2,1,0:T(8,128)(2,1)}, bf16[8,512,1024]{2,1,0:T(8,128)(2,1)}) fusion(bf16[8,512,2048]{2,1,0:T(8,128)(2,1)S(1)} %bitcast_dynamic-update-slice_fusion.2), kind=kLoop, calls=%fused_computation.123 | loop fusion | bytes 33554432 | tf_op jit(solution)/shard_map/gather | solution.py:37
  290.6 8.1 %gather_fusion.3 = bf16[8,512,1024]{2,1,0:T(8,128)(2,1)} fusion(bf16[8,512,1024]{2,1,0:T(8,128)(2,1)} %get-tuple-element.106, s32[1024]{0:T(1024)S(1)} %get-tuple-element.118), kind=kCustom, calls=%fused_computation.5 | custom fusion | bytes 16777248 | tf_op jit(solution)/shard_map/gather | solution.py:37
  298.7 8.3 %gather_fusion.4 = bf16[8,512,1024]{2,1,0:T(8,128)(2,1)} fusion(bf16[8,512,1024]{2,1,0:T(8,128)(2,1)} %get-tuple-element.107, s32[1024]{0:T(1024)S(1)} %get-tuple-element.118), kind=kCustom, calls=%fused_computation.6 | custom fusion | bytes 16777248 | tf_op jit(solution)/shard_map/gather | solution.py:37
  307.1 8.2 %pad_maximum_fusion = bf16[8,512,2048]{2,1,0:T(8,128)(2,1)S(1)} fusion(bf16[8,512,1024]{2,1,0:T(8,128)(2,1)} %gather_fusion.4, bf16[8,512,1024]{2,1,0:T(8,128)(2,1)} %gather_fusion.3), kind=kLoop, calls=%fused_computation.26 | loop fusion | flops 33554432 | bytes 33554432
  315.3 4.7 fusion.26
  326.9 2.5 copy.105
  329.4 2.7 reshape.269
  332.2 2.9 fusion.20
  335.1 3.1 gather_fusion.1
  338.7 4.8 broadcast_select_fusion
  343.5 18.7 %all-gather.8.cloned.1.call-done = bf16[8,2048,256]{2,1,0:T(8,128)(2,1)} async-done(((bf16[1,2048,256]{2,1,0:T(8,128)(2,1)}), bf16[8,2048,256]{2,1,0:T(8,128)(2,1)}) %all-gather.8.cloned.1.call-update) | async-done | bytes 8388624 | tf_op jit(solution)/shard_map/all_gather | solution.py:179
  362.1 183.7 %while.14 = (s32[]{:T(128)}, f32[8,2,64,2048]{3,2,1,0:T(8,128)}, f32[8,2,64,16]{2,3,1,0:T(8,128)S(1)}, f32[8,2,64,16]{2,3,1,0:T(8,128)S(1)}, bf16[8,2048,256]{2,...) while((s32[]{:T(128)}, f32[8,2,64,2048]{3,2,1,0:T(8,128)}, ...), condition=%wide.region_7.8_spmd, body=%wide.region_4.7_spmd.sunk | while | flops 2193620992 | bytes 136962704 | solution.py:190
  365.2 2.8 fusion.74
  368.0 3.8 fusion.76
  375.7 7.6 %fusion.75 = f32[2,64,2,8,128]{4,1,3,0,2:T(8,128)S(1)} fusion(bf16[2048,2,128,1,1]{0,2,4,3,1:T(8,128)(2,1)S(1)} %bitcast.161, f32[2,2048,2,64,8]{1,3,4,2,0:T(8,128)} %copy-done, f32[2,64,2,8]{1,3,0,2:T(8,128)S(1)} %get-tuple-element.173, pred[2,2048]{1,0:T(4,128)(4,1)S(1)} %compare_bitcast_fusion.2), kind=kOutput, calls=%fused_computation.14.clone.1 | convolution fusion | flops 1090519040 | bytes 18886656 | tf_op jit(solution)/shard_map/while/body/eval_jaxpr/vmap(tkgl,lkd->tkgd)/dot_general | solution.py:78
  388.2 2.8 fusion.74
  390.9 3.8 fusion.76
  398.6 7.6 %fusion.75 = f32[2,64,2,8,128]{4,1,3,0,2:T(8,128)S(1)} fusion(bf16[2048,2,128,1,1]{0,2,4,3,1:T(8,128)(2,1)S(1)} %bitcast.161, f32[2,2048,2,64,8]{1,3,4,2,0:T(8,128)} %copy-done, f32[2,64,2,8]{1,3,0,2:T(8,128)S(1)} %get-tuple-element.173, pred[2,2048]{1,0:T(4,128)(4,1)S(1)} %compare_bitcast_fusion.2), kind=kOutput, calls=%fused_computation.14.clone.1 | convolution fusion | flops 1090519040 | bytes 18886656 | tf_op jit(solution)/shard_map/while/body/eval_jaxpr/vmap(tkgl,lkd->tkgd)/dot_general | solution.py:78
  411.1 2.8 fusion.74
  413.9 3.8 fusion.76
  421.6 7.6 %fusion.75 = f32[2,64,2,8,128]{4,1,3,0,2:T(8,128)S(1)} fusion(bf16[2048,2,128,1,1]{0,2,4,3,1:T(8,128)(2,1)S(1)} %bitcast.161, f32[2,2048,2,64,8]{1,3,4,2,0:T(8,128)} %copy-done, f32[2,64,2,8]{1,3,0,2:T(8,128)S(1)} %get-tuple-element.173, pred[2,2048]{1,0:T(4,128)(4,1)S(1)} %compare_bitcast_fusion.2), kind=kOutput, calls=%fused_computation.14.clone.1 | convolution fusion | flops 1090519040 | bytes 18886656 | tf_op jit(solution)/shard_map/while/body/eval_jaxpr/vmap(tkgl,lkd->tkgd)/dot_general | solution.py:78
  434.0 2.8 fusion.74
  436.8 3.8 fusion.76
  444.5 7.6 %fusion.75 = f32[2,64,2,8,128]{4,1,3,0,2:T(8,128)S(1)} fusion(bf16[2048,2,128,1,1]{0,2,4,3,1:T(8,128)(2,1)S(1)} %bitcast.161, f32[2,2048,2,64,8]{1,3,4,2,0:T(8,128)} %copy-done, f32[2,64,2,8]{1,3,0,2:T(8,128)S(1)} %get-tuple-element.173, pred[2,2048]{1,0:T(4,128)(4,1)S(1)} %compare_bitcast_fusion.2), kind=kOutput, calls=%fused_computation.14.clone.1 | convolution fusion | flops 1090519040 | bytes 18886656 | tf_op jit(solution)/shard_map/while/body/eval_jaxpr/vmap(tkgl,lkd->tkgd)/dot_general | solution.py:78
  457.0 2.8 fusion.74
  459.8 3.8 fusion.76
  467.5 7.6 %fusion.75 = f32[2,64,2,8,128]{4,1,3,0,2:T(8,128)S(1)} fusion(bf16[2048,2,128,1,1]{0,2,4,3,1:T(8,128)(2,1)S(1)} %bitcast.161, f32[2,2048,2,64,8]{1,3,4,2,0:T(8,128)} %copy-done, f32[2,64,2,8]{1,3,0,2:T(8,128)S(1)} %get-tuple-element.173, pred[2,2048]{1,0:T(4,128)(4,1)S(1)} %compare_bitcast_fusion.2), kind=kOutput, calls=%fused_computation.14.clone.1 | convolution fusion | flops 1090519040 | bytes 18886656 | tf_op jit(solution)/shard_map/while/body/eval_jaxpr/vmap(tkgl,lkd->tkgd)/dot_general | solution.py:78
  480.0 2.8 fusion.74
  482.7 3.8 fusion.76
  490.4 7.6 %fusion.75 = f32[2,64,2,8,128]{4,1,3,0,2:T(8,128)S(1)} fusion(bf16[2048,2,128,1,1]{0,2,4,3,1:T(8,128)(2,1)S(1)} %bitcast.161, f32[2,2048,2,64,8]{1,3,4,2,0:T(8,128)} %copy-done, f32[2,64,2,8]{1,3,0,2:T(8,128)S(1)} %get-tuple-element.173, pred[2,2048]{1,0:T(4,128)(4,1)S(1)} %compare_bitcast_fusion.2), kind=kOutput, calls=%fused_computation.14.clone.1 | convolution fusion | flops 1090519040 | bytes 18886656 | tf_op jit(solution)/shard_map/while/body/eval_jaxpr/vmap(tkgl,lkd->tkgd)/dot_general | solution.py:78
  502.9 2.8 fusion.74
  505.7 3.8 fusion.76
  513.4 7.6 %fusion.75 = f32[2,64,2,8,128]{4,1,3,0,2:T(8,128)S(1)} fusion(bf16[2048,2,128,1,1]{0,2,4,3,1:T(8,128)(2,1)S(1)} %bitcast.161, f32[2,2048,2,64,8]{1,3,4,2,0:T(8,128)} %copy-done, f32[2,64,2,8]{1,3,0,2:T(8,128)S(1)} %get-tuple-element.173, pred[2,2048]{1,0:T(4,128)(4,1)S(1)} %compare_bitcast_fusion.2), kind=kOutput, calls=%fused_computation.14.clone.1 | convolution fusion | flops 1090519040 | bytes 18886656 | tf_op jit(solution)/shard_map/while/body/eval_jaxpr/vmap(tkgl,lkd->tkgd)/dot_general | solution.py:78
  525.9 2.8 fusion.74
  528.7 3.8 fusion.76
  536.4 7.6 %fusion.75 = f32[2,64,2,8,128]{4,1,3,0,2:T(8,128)S(1)} fusion(bf16[2048,2,128,1,1]{0,2,4,3,1:T(8,128)(2,1)S(1)} %bitcast.161, f32[2,2048,2,64,8]{1,3,4,2,0:T(8,128)} %copy-done, f32[2,64,2,8]{1,3,0,2:T(8,128)S(1)} %get-tuple-element.173, pred[2,2048]{1,0:T(4,128)(4,1)S(1)} %compare_bitcast_fusion.2), kind=kOutput, calls=%fused_computation.14.clone.1 | convolution fusion | flops 1090519040 | bytes 18886656 | tf_op jit(solution)/shard_map/while/body/eval_jaxpr/vmap(tkgl,lkd->tkgd)/dot_general | solution.py:78
  547.7 4.2 gather_fusion.2
  554.7 4.4 fusion.16
  (221 shorter events, 101.3 us)
Async XLA Ops:
  6.5 2.9 copy-start.7
  6.5 97.5 %copy-start.19 = (s32[4]{0:T(128)S(1)}, s32[4]{0:T(128)}, u32[]{:S(2)}) copy-start(s32[4]{0:T(128)} %param.26) | copy-start | bytes 52
  6.5 97.9 %copy-start.1 = (s32[4]{0:T(128)S(1)}, s32[4]{0:T(128)}, u32[]{:S(2)}) copy-start(s32[4]{0:T(128)} %param.27) | copy-start | bytes 52
  6.5 177.4 %all-gather.10.cloned.1.call-start = ((), (), s32[]{:S(2)}) async-start(), calls=%async_computation.2 | async-start | bytes 2621440 | tf_op jit(solution)/shard_map/all_gather | solution.py:124
  7.3 178.9 %all-gather.12.cloned.1.call-start = ((), (), s32[]{:S(2)}) async-start(), calls=%async_computation.3 | async-start | bytes 2359296 | tf_op jit(solution)/shard_map/all_gather | solution.py:129
  8.0 180.8 %all-gather.14.cloned.1.call-start = ((), (), s32[]{:S(2)}) async-start(), calls=%async_computation.4 | async-start | bytes 2359296 | tf_op jit(solution)/shard_map/all_gather | solution.py:134
  8.7 334.7 %all-gather.6.cloned.1.call-start = ((), (), s32[]{:S(2)}) async-start(), calls=%async_computation | async-start | bytes 9437184 | tf_op jit(solution)/shard_map/all_gather | solution.py:180
  9.3 176.9 %copy-start.20 = (f32[4096]{0:T(1024)S(1)}, f32[4096]{0:T(1024)}, u32[]{:S(2)}) copy-start(f32[4096]{0:T(1024)} %param.17) | copy-start | bytes 49156
  9.3 176.9 %copy-start.22 = (f32[256]{0:T(256)S(1)}, f32[256]{0:T(256)}, u32[]{:S(2)}) copy-start(f32[256]{0:T(256)} %param.22) | copy-start | bytes 3076
  9.3 352.8 %all-gather.8.cloned.1.call-start = ((), (), s32[]{:S(2)}) async-start(), calls=%async_computation.1 | async-start | bytes 9437184 | tf_op jit(solution)/shard_map/all_gather | solution.py:179
  9.4 28.4 %collective-permute-start = (bf16[512,2048]{1,0:T(8,128)(2,1)S(1)}, bf16[512,2048]{1,0:T(8,128)(2,1)}, u32[]{:S(2)}, u32[]{:S(2)}) collective-permute-start(bf16[512,2048]{1,0:T(8,128)(2,1)S(1)} %copy-done.7), channel_id=1, source_target_pairs={{0,1},{1,2},{2,3},{3,4},{4,5},{5,6},{6,7},{7,0},{8,9},{9,10},{10,1... | collective-permute-start | bytes 6291464 | tf_op jit(solution)/shard_map/ppermute | solution.py:30
  37.8 66.3 %collective-permute-start.1 = (bf16[512,2048]{1,0:T(8,128)(2,1)}, bf16[512,2048]{1,0:T(8,128)(2,1)}, u32[]{:S(2)}, u32[]{:S(2)}) collective-permute-start(bf16[512,2048]{1,0:T(8,128)(2,1)} %collective-permute-done), channel_id=1, source_target_pairs={{0,1},{1,2},{2,3},{3,4},{4,5},{5,6},{6,7},{7,0},{8,9},{9,10},{10,1... | collective-permute-start | bytes 6291464 | tf_op jit(solution)/shard_map/ppermute | solution.py:30
  37.8 70.4 %collective-permute-start.4 = (bf16[512,2048]{1,0:T(8,128)(2,1)S(1)}, bf16[512,2048]{1,0:T(8,128)(2,1)}, u32[]{:S(2)}, u32[]{:S(2)}) collective-permute-start(bf16[512,2048]{1,0:T(8,128)(2,1)S(1)} %copy-done.7), channel_id=1, source_target_pairs={{1,0},{2,1},{3,2},{4,3},{5,4},{6,5},{7,6},{0,7},{9,8},{10,9},{11,1... | collective-permute-start | bytes 6291464 | tf_op jit(solution)/shard_map/ppermute | solution.py:33
  104.0 79.7 %collective-permute-start.2 = (bf16[512,2048]{1,0:T(8,128)(2,1)}, bf16[512,2048]{1,0:T(8,128)(2,1)}, u32[]{:S(2)}, u32[]{:S(2)}) collective-permute-start(bf16[512,2048]{1,0:T(8,128)(2,1)} %collective-permute-done.1), channel_id=1, source_target_pairs={{0,1},{1,2},{2,3},{3,4},{4,5},{5,6},{6,7},{7,0},{8,9},{9,10},{10,1... | collective-permute-start | bytes 6291464 | tf_op jit(solution)/shard_map/ppermute | solution.py:30
  104.2 2.6 copy-start.13
  105.4 1.4 copy-start.17
  108.2 84.0 %collective-permute-start.5 = (bf16[512,2048]{1,0:T(8,128)(2,1)}, bf16[512,2048]{1,0:T(8,128)(2,1)}, u32[]{:S(2)}, u32[]{:S(2)}) collective-permute-start(bf16[512,2048]{1,0:T(8,128)(2,1)} %collective-permute-done.4), channel_id=1, source_target_pairs={{1,0},{2,1},{3,2},{4,3},{5,4},{6,5},{7,6},{0,7},{9,8},{10,9},{11,1... | collective-permute-start | bytes 6291464 | tf_op jit(solution)/shard_map/ppermute | solution.py:33
  183.7 87.9 %collective-permute-start.3 = (bf16[512,2048]{1,0:T(8,128)(2,1)}, bf16[512,2048]{1,0:T(8,128)(2,1)}, u32[]{:S(2)}, u32[]{:S(2)}) collective-permute-start(bf16[512,2048]{1,0:T(8,128)(2,1)} %collective-permute-done.2), channel_id=1, source_target_pairs={{0,1},{1,2},{2,3},{3,4},{4,5},{5,6},{6,7},{7,0},{8,9},{9,10},{10,1... | collective-permute-start | bytes 6291464 | tf_op jit(solution)/shard_map/ppermute | solution.py:30
  183.9 2.3 copy-start.9
  186.2 2.6 copy-start.23
  192.1 91.0 %collective-permute-start.6 = (bf16[512,2048]{1,0:T(8,128)(2,1)}, bf16[512,2048]{1,0:T(8,128)(2,1)S(1)}, u32[]{:S(2)}, u32[]{:S(2)}) collective-permute-start(bf16[512,2048]{1,0:T(8,128)(2,1)} %collective-permute-done.5), channel_id=1, source_target_pairs={{1,0},{2,1},{3,2},{4,3},{5,4},{6,5},{7,6},{0,7},{9,8},{10,9},{11,1... | collective-permute-start | bytes 6291464 | tf_op jit(solution)/shard_map/ppermute | solution.py:33
  277.1 2.2 copy-start.8
  307.1 8.2 %copy-start.10 = (bf16[256,4096]{1,0:T(8,128)(2,1)S(1)}, bf16[256,4096]{1,0:T(8,128)(2,1)}, u32[]{:S(2)}) copy-start(bf16[256,4096]{1,0:T(8,128)(2,1)} %all-gather.10.cloned.1.call-done) | copy-start | bytes 6291460
  307.1 8.2 %copy-start.21 = (f32[2048]{0:T(1024)S(1)}, f32[2048]{0:T(1024)}, u32[]{:S(2)}) copy-start(f32[2048]{0:T(1024)} %param.21) | copy-start | bytes 24580
  321.1 1.3 copy-start.4
  321.1 2.0 copy-start.5
  325.5 1.4 copy-start.2
  335.1 3.1 copy-start.3
  338.7 23.4 %copy-start.11 = (f32[8,2,64,16]{2,3,1,0:T(8,128)S(1)}, f32[8,2,64,16]{2,3,1,0:T(8,128)}, u32[]{:S(2)}) copy-start(f32[8,2,64,16]{2,3,1,0:T(8,128)} %custom-call.16) | copy-start | bytes 196612
  338.7 23.4 %copy-start.12 = (f32[8,2,64,16]{2,3,1,0:T(8,128)S(1)}, f32[8,2,64,16]{2,3,1,0:T(8,128)}, u32[]{:S(2)}) copy-start(f32[8,2,64,16]{2,3,1,0:T(8,128)} %custom-call.17) | copy-start | bytes 196612
  362.1 185.1 %copy-start.14 = (pred[4]{0:T(512)(128)(4,1)S(1)}, pred[4]{0:T(512)(128)(4,1)}, u32[]{:S(2)}) copy-start(pred[4]{0:T(512)(128)(4,1)} %copy-done.13) | copy-start | bytes 16
  362.1 185.1 %copy-start.18 = (pred[4]{0:T(512)(128)(4,1)S(1)}, pred[4]{0:T(512)(128)(4,1)}, u32[]{:S(2)}) copy-start(pred[4]{0:T(512)(128)(4,1)} %copy-done.17) | copy-start | bytes 16
  368.0 5.8 %copy-start = (f32[2,2048,2,64,8]{1,3,4,2,0:T(8,128)}, f32[2,2048,2,64,8]{1,3,4,2,0:T(8,128)S(1)}, u32[]{:S(2)}) copy-start(f32[2,2048,2,64,8]{1,3,4,2,0:T(8,128)S(1)} %get-tuple-element.172) | copy-start | bytes 50331652 | tf_op jit(solution)/shard_map/while
  390.9 5.8 %copy-start = (f32[2,2048,2,64,8]{1,3,4,2,0:T(8,128)}, f32[2,2048,2,64,8]{1,3,4,2,0:T(8,128)S(1)}, u32[]{:S(2)}) copy-start(f32[2,2048,2,64,8]{1,3,4,2,0:T(8,128)S(1)} %get-tuple-element.172) | copy-start | bytes 50331652 | tf_op jit(solution)/shard_map/while
  413.9 5.8 %copy-start = (f32[2,2048,2,64,8]{1,3,4,2,0:T(8,128)}, f32[2,2048,2,64,8]{1,3,4,2,0:T(8,128)S(1)}, u32[]{:S(2)}) copy-start(f32[2,2048,2,64,8]{1,3,4,2,0:T(8,128)S(1)} %get-tuple-element.172) | copy-start | bytes 50331652 | tf_op jit(solution)/shard_map/while
  436.8 5.8 %copy-start = (f32[2,2048,2,64,8]{1,3,4,2,0:T(8,128)}, f32[2,2048,2,64,8]{1,3,4,2,0:T(8,128)S(1)}, u32[]{:S(2)}) copy-start(f32[2,2048,2,64,8]{1,3,4,2,0:T(8,128)S(1)} %get-tuple-element.172) | copy-start | bytes 50331652 | tf_op jit(solution)/shard_map/while
  459.8 5.8 %copy-start = (f32[2,2048,2,64,8]{1,3,4,2,0:T(8,128)}, f32[2,2048,2,64,8]{1,3,4,2,0:T(8,128)S(1)}, u32[]{:S(2)}) copy-start(f32[2,2048,2,64,8]{1,3,4,2,0:T(8,128)S(1)} %get-tuple-element.172) | copy-start | bytes 50331652 | tf_op jit(solution)/shard_map/while
  482.7 5.8 %copy-start = (f32[2,2048,2,64,8]{1,3,4,2,0:T(8,128)}, f32[2,2048,2,64,8]{1,3,4,2,0:T(8,128)S(1)}, u32[]{:S(2)}) copy-start(f32[2,2048,2,64,8]{1,3,4,2,0:T(8,128)S(1)} %get-tuple-element.172) | copy-start | bytes 50331652 | tf_op jit(solution)/shard_map/while
  505.7 5.8 %copy-start = (f32[2,2048,2,64,8]{1,3,4,2,0:T(8,128)}, f32[2,2048,2,64,8]{1,3,4,2,0:T(8,128)S(1)}, u32[]{:S(2)}) copy-start(f32[2,2048,2,64,8]{1,3,4,2,0:T(8,128)S(1)} %get-tuple-element.172) | copy-start | bytes 50331652 | tf_op jit(solution)/shard_map/while
  528.6 5.8 %copy-start = (f32[2,2048,2,64,8]{1,3,4,2,0:T(8,128)}, f32[2,2048,2,64,8]{1,3,4,2,0:T(8,128)S(1)}, u32[]{:S(2)}) copy-start(f32[2,2048,2,64,8]{1,3,4,2,0:T(8,128)S(1)} %get-tuple-element.172) | copy-start | bytes 50331652 | tf_op jit(solution)/shard_map/while
  553.1 1.6 copy-start.6
  553.1 1.6 copy-start.15
  553.1 1.6 copy-start.16
Sparse Core Ops, SparseCore 0:
  9.2 38.0 all-gather.9
  48.9 41.9 all-gather.11
  92.5 43.0 all-gather.13
  137.0 136.1 all-gather.5
  274.6 87.4 all-gather.7
